TPU v7x, 256 devices: a whole 4x4x8 slice. The times are simulated.
256 devices in a mesh: tab: 64 (over y, z, core), col: 4 (over x).
Axes of the slice: x: 4, y: 4, z: 8, core: 2. Of those that a mesh axis runs over, the one named last changes fastest.
Arguments:
- bag_items: bfloat16 [128, 4, 48, 8192], P('tab', None, 'col'), may hold values from -3 to 3
- lengths: int32 [128, 8192], P('tab'), may hold values from 1 to 4
- field_slot: int32 [64], replicated, may hold values from 0 to 127, as said below
- filter_one: bfloat16 [32, 4096], replicated, may hold values from -0.09375 to 0.09375
- filter_two: bfloat16 [32, 2048], replicated, may hold values from -0.125 to 0.125
- cotangent: bfloat16 [64, 8192], P(None, ('tab', 'col')), may hold values from -12 to 12
Outputs:
- pooled: float32 [64, 8192], P(None, ('tab', 'col'))
- filter_grad_one: float32 [32, 4096], P(None, ('tab', 'col'))
- filter_grad_two: float32 [32, 2048], P(None, ('tab', 'col'))
- pooled_grad: bfloat16 [128, 48, 8192], P('tab', 'col')
Inputs may be any that keep to these rules, and one draw needn't show every extreme that they name: Distinct values; the table of field f is held by index field_slot[f] // 2 of tab; owners hold 0 to 2 fields and one owner holds 2.
All inputs are finite; a program needn't handle non-finite values.
Results may differ from a plain program's by a relative error of at most 0.017.
Values may be sent and summed in bfloat16 or wider, within the bound.
A program may use at most 64 MiB of HBM per device.

v0:
```python
import math

import jax
import jax.numpy as jnp
from jax import lax
from jax.sharding import PartitionSpec as P

D = 48


def cross_block(first_cols, upstream, filter_one, filter_two):
    fields, columns = first_cols.shape
    map_count = filter_one.shape[0]
    first_pairs = (first_cols[:, None, :] * first_cols[None, :, :]).reshape(
        fields * fields, columns
    )
    first_maps = jnp.dot(filter_one, first_pairs, preferred_element_type=jnp.float32)
    hidden_cols = lax.optimization_barrier(first_maps.astype(jnp.bfloat16))
    second_pairs = (hidden_cols[:, None, :] * first_cols[None, :, :]).reshape(
        map_count * fields, columns
    )
    second_maps = jnp.dot(filter_two, second_pairs, preferred_element_type=jnp.float32)
    upper_grad = upstream[map_count:]
    grad_two = lax.dot_general(
        upper_grad, second_pairs, (((1,), (1,)), ((), ())), preferred_element_type=jnp.float32
    )
    pair_grad_two = lax.dot_general(
        filter_two, upper_grad, (((0,), (0,)), ((), ())), preferred_element_type=jnp.float32
    )
    pair_grad_two = lax.optimization_barrier(pair_grad_two.astype(jnp.bfloat16))
    pair_grad_two = pair_grad_two.reshape(map_count, fields, columns).astype(jnp.float32)
    first_float = first_cols.astype(jnp.float32)
    hidden_grad = jnp.sum(pair_grad_two * first_float[None], axis=1)
    field_grad = jnp.sum(pair_grad_two * hidden_cols.astype(jnp.float32)[:, None], axis=0)
    lower_grad = (upstream[:map_count].astype(jnp.float32) + hidden_grad).astype(jnp.bfloat16)
    grad_one = lax.dot_general(
        lower_grad, first_pairs, (((1,), (1,)), ((), ())), preferred_element_type=jnp.float32
    )
    pair_grad_one = lax.dot_general(
        filter_one, lower_grad, (((0,), (0,)), ((), ())), preferred_element_type=jnp.float32
    )
    pair_grad_one = lax.optimization_barrier(pair_grad_one.astype(jnp.bfloat16))
    pair_grad_one = pair_grad_one.reshape(fields, fields, columns).astype(jnp.float32)
    field_grad = (
        field_grad
        + jnp.sum(pair_grad_one * first_float[None], axis=1)
        + jnp.sum(pair_grad_one * first_float[:, None], axis=0)
    )
    return (first_maps, second_maps, field_grad.astype(jnp.bfloat16), grad_one, grad_two)


def cross_layers(embed_rows, upstream, filter_one, filter_two):
    fields, columns = embed_rows.shape
    map_count = filter_one.shape[0]
    block_cols = math.gcd(columns, 512)
    block_count = columns // block_cols
    embed_blocks = embed_rows.reshape(fields, block_count, block_cols).transpose(1, 0, 2)
    grad_blocks = upstream.reshape(2 * map_count, block_count, block_cols).transpose(1, 0, 2)

    def advance(totals, inputs):
        first_maps, second_maps, field_grad, grad_one, grad_two = cross_block(
            inputs[0], inputs[1], filter_one, filter_two
        )
        both_maps = jnp.concatenate([first_maps, second_maps], axis=0)
        return ((totals[0] + grad_one, totals[1] + grad_two), (both_maps, field_grad))

    zero_sums = (jnp.zeros(filter_one.shape, jnp.float32), jnp.zeros(filter_two.shape, jnp.float32))
    (grad_one, grad_two), (map_blocks, field_blocks) = lax.scan(
        advance, zero_sums, (embed_blocks, grad_blocks)
    )
    both_maps = map_blocks.transpose(1, 0, 2).reshape(2 * map_count, columns)
    field_grad = field_blocks.transpose(1, 0, 2).reshape(fields, columns)
    return (both_maps, field_grad, grad_one, grad_two)


def per_device(bag_items, lengths, field_slot, filter_one, filter_two, cotangent):
    slot_count, item_count, col_width, samples = bag_items.shape
    tab_count = lax.axis_size("tab")
    item_index = jnp.arange(item_count)[None, :, None, None]
    kept_items = jnp.where(
        item_index < lengths[:, None, None, :], bag_items, jnp.zeros_like(bag_items)
    )
    pooled_table = jnp.sum(kept_items, axis=1, dtype=jnp.float32).astype(jnp.bfloat16)
    per_owner = pooled_table.reshape(slot_count, col_width, tab_count, samples // tab_count)
    received = lax.all_to_all(per_owner, "tab", split_axis=2, concat_axis=0, tiled=True)
    grad_rows = lax.all_gather(cotangent, "col", axis=1, tiled=True)
    all_slots = received.shape[0]
    local_width = received.shape[1]
    local_samples = received.shape[3]
    slot_rows = received.reshape(all_slots, local_width * local_samples)
    embed_rows = jnp.take(slot_rows, field_slot, axis=0)
    grad_count = grad_rows.shape[0]
    upstream = jnp.broadcast_to(
        grad_rows[:, None, :], (grad_count, local_width, local_samples)
    ).astype(jnp.float32) * D ** (-0.5)
    upstream = upstream.astype(jnp.bfloat16).reshape(grad_count, local_width * local_samples)
    both_maps, field_grad, grad_one, grad_two = cross_layers(
        embed_rows, upstream, filter_one, filter_two
    )
    pooled_part = jnp.sum(
        both_maps.reshape(grad_count, local_width, local_samples), axis=1
    ) * D ** (-0.5)
    grad_table = jnp.zeros_like(slot_rows).at[field_slot].set(field_grad).reshape(received.shape)
    pooled = lax.psum_scatter(pooled_part, "col", scatter_dimension=1, tiled=True)
    returned = lax.all_to_all(grad_table, "tab", split_axis=0, concat_axis=2, tiled=True)
    pooled_grad = returned.reshape(slot_count, col_width, samples)
    grad_scale = samples ** (-0.5)
    grad_one, grad_two = (
        lax.psum_scatter(grad_one * grad_scale, ("tab", "col"), scatter_dimension=1, tiled=True),
        lax.psum_scatter(grad_two * grad_scale, ("tab", "col"), scatter_dimension=1, tiled=True),
    )
    return (pooled, grad_one, grad_two, pooled_grad)


def solution(mesh):
    in_specs = (P("tab", None, "col", None), P("tab", None), P(), P(), P(), P(None, ("tab", "col")))
    out_specs = (
        P(None, ("tab", "col")),
        P(None, ("tab", "col")),
        P(None, ("tab", "col")),
        P("tab", "col", None),
    )
    return jax.shard_map(
        per_device, mesh=mesh, in_specs=in_specs, out_specs=out_specs, check_vma=False
    )
```

profile of v0, /device:TPU:1, one launch (start us, length us, event | category | flops | bytes accessed | tf_op | source)
XLA Modules:
  0.0 1469.2 jit_solution(11257829453116824667)
XLA Ops:
  8.0 0.9 iota_compare_fusion
  8.9 3.2 select_reduce_fusion
  12.5 1.1 copy.91
  13.7 13.1 all-to-all-start
  26.9 10.3 all_gather.3
  37.5 0.7 copy.93
  38.2 3.1 all-to-all-done
  41.6 0.7 gather_fusion
  42.6 0.7 copy.94
  43.4 107.2 %while.17 = (s32[]{:T(128)}, f32[32,4096]{1,0:T(8,128)S(1)}, f32[32,2048]{1,0:T(8,128)S(1)}, f32[3,64,512]{2,1,0:T(8,128)}, bf16[3,64,512]{2,1,0:T(8,128)(2,1)},...) while((s32[]{:T(128)}, f32[32,4096]{1,0:T(8,128)S(1)}, ...), condition=%wide.region_6.7_spmd.clone, body=%wide.region_1.6_spmd.clone.sunk | while | flops 623427584 | bytes 108364040 | solution.py:68
  43.4 0.9 fusion.55
  44.2 2.2 broadcast_multiply_fusion.7
  46.4 1.5 fusion.56
  47.9 3.0 copy.115
  50.9 3.0 multiply_reduce_fusion.7
  54.4 1.3 convolution_add_fusion.4
  55.7 0.8 fusion.57
  56.7 0.7 convolution_add_fusion.5
  57.4 0.5 convolution_bitcast_fusion.3
  57.9 0.7 fusion.58
  58.6 3.2 fusion.59
  61.8 7.1 copy.116
  68.9 8.8 multiply_reduce_fusion.8
  77.8 0.7 multiply_reduce_fusion.9
  78.4 0.7 fusion.60
  79.1 0.9 fusion.55
  80.0 2.2 broadcast_multiply_fusion.7
  82.2 1.5 fusion.56
  83.6 3.0 copy.115
  86.7 3.0 multiply_reduce_fusion.7
  90.1 1.3 convolution_add_fusion.4
  91.5 0.8 fusion.57
  92.4 0.7 convolution_add_fusion.5
  93.6 0.7 fusion.58
  94.3 3.2 fusion.59
  97.5 7.1 copy.116
  104.6 8.8 multiply_reduce_fusion.8
  113.5 0.7 multiply_reduce_fusion.9
  114.2 0.7 fusion.60
  114.8 0.9 fusion.55
  115.7 2.2 broadcast_multiply_fusion.7
  117.9 1.5 fusion.56
  119.4 3.0 copy.115
  122.4 3.0 multiply_reduce_fusion.7
  125.9 1.3 convolution_add_fusion.4
  127.2 0.8 fusion.57
  128.2 0.7 convolution_add_fusion.5
  129.4 0.7 fusion.58
  130.0 3.2 fusion.59
  133.3 7.1 copy.116
  140.4 8.8 multiply_reduce_fusion.8
  149.2 0.7 multiply_reduce_fusion.9
  149.9 0.7 fusion.60
  150.6 1.3 copy.95
  152.1 1.3 copy.96
  153.6 0.7 copy.105
  154.5 2.0 copy.107
  156.5 1.0 scatter_custom_fusion
  157.8 1.2 copy.99
  158.9 9.4 all-to-all-start.1
  168.3 244.3 %all-reduce.3.cloned.1.call-done = f32[32,2048]{0,1:T(8,128)} async-done(((f32[32,2048]{0,1:T(8,128)}), f32[32,2048]{0,1:T(8,128)}) %all-reduce.3.cloned.1.call-update) | async-done | bytes 262160
  412.7 1.3 constant_dynamic-slice_fusion
  413.9 0.8 copy.100
  414.8 1047.0 %reduce-scatter.9.cloned.1.call-done = f32[16,32]{1,0:T(8,128)} async-done(((f32[4096,32]{1,0:T(8,128)}), f32[16,32]{1,0:T(8,128)}) %reduce-scatter.9.cloned.1.call-update) | async-done | bytes 2064
  (67 shorter events, 4.6 us)
Async XLA Ops:
  8.0 18.9 %copy-start.6 = (bf16[64,32]{0,1:T(8,128)(2,1)S(1)}, bf16[64,32]{0,1:T(8,128)(2,1)}, u32[]{:S(2)}) copy-start(bf16[64,32]{0,1:T(8,128)(2,1)} %param.13) | copy-start | bytes 12292
  8.0 30.2 %copy-start.7 = (s32[64]{0:T(128)S(1)}, s32[64]{0:T(128)}, u32[]{:S(2)}) copy-start(s32[64]{0:T(128)} %param.10) | copy-start | bytes 772
  12.5 30.9 %copy-start.2 = (bf16[32,4096]{1,0:T(8,128)(2,1)S(1)}, bf16[32,4096]{1,0:T(8,128)(2,1)}, u32[]{:S(2)}) copy-start(bf16[32,4096]{1,0:T(8,128)(2,1)} %param.11) | copy-start | bytes 786436
  12.5 30.9 %copy-start.3 = (bf16[32,2048]{1,0:T(8,128)(2,1)S(1)}, bf16[32,2048]{1,0:T(8,128)(2,1)}, u32[]{:S(2)}) copy-start(bf16[32,2048]{1,0:T(8,128)(2,1)} %param.12) | copy-start | bytes 393220
  13.7 27.7 %all-to-all-start = ((bf16[2,12,64,128]{3,0,1,2:T(2,128)(2,1)}), bf16[2,12,64,128]{3,0,1,2:T(2,128)(2,1)S(1)}, u32[]{:S(2)}, u32[]{:S(2)}) async-start(bf16[2,12,64,128]{3,0,1,2:T(2,128)(2,1)} %copy.91), calls=%async_computation | async-start | bytes 786432 | tf_op jit(solution)/shard_map/all_to_all | solution.py:85
  26.8 385.9 %all-reduce.3.cloned.1.call-start = ((), (), s32[]{:S(2)}) async-start(), calls=%async_computation.6 | async-start | bytes 2097152
  50.9 3.4 copy-start.1
  50.9 3.4 copy-start.4
  68.9 8.9 copy-start
  86.7 3.4 copy-start.1
  86.7 3.4 copy-start.4
  104.6 8.9 copy-start
  122.4 3.4 copy-start.1
  122.4 3.4 copy-start.4
  140.4 8.9 copy-start
  152.1 4.4 copy-start.5
  153.5 261.3 %reduce-scatter.7.cloned.1.call-start = ((), (), s32[]{:S(2)}) async-start(), calls=%async_computation.4 | async-start | bytes 81920
  154.4 1307.4 %reduce-scatter.9.cloned.1.call-start = ((), (), s32[]{:S(2)}) async-start(), calls=%async_computation.5 | async-start | bytes 2105344
  158.9 255.0 %all-to-all-start.1 = ((bf16[128,12,1,128]{3,1,2,0:T(8,128)(2,1)}), bf16[128,12,1,128]{3,1,2,0:T(8,128)(2,1)S(1)}, u32[]{:S(2)}, u32[]{:S(2)}) async-start(bf16[128,12,1,128]{3,1,2,0:T(8,128)(2,1)} %copy.99), calls=%async_computation.1 | async-start | bytes 1048576 | tf_op jit(solution)/shard_map/all_to_all | solution.py:105
Sparse Core Ops, SparseCore 0:
  153.6 259.0 all-reduce.2
Sparse Core Ops, SparseCore 1:
  157.0 20.8 reduce-scatter.6
  180.8 1281.0 reduce-scatter.8
where the time goes:
time: 1480 us; the launch traced here: 1470 us
  waiting for transfers between devices  1290 us (87%)
  other arithmetic  55.8 us (4%)
  local copies, waits for them, and re-layouts  45.9 us (3%)
  matrix products  24.1 us (2%)
  starting transfers between devices  22.6 us (2%)
  between operations  15.7 us (1%)
    unnamed x6, waiting for transfers between devices  1290 us
  transfers between devices with their start and end apart: 5, of which 3 were waited for; matrix products, arithmetic and copies ran while one was open for 1% of the time, Pallas kernels for 0%

commit v1 on v0

v1 whole, which is shorter than its diff:
```python
import functools

import jax
import jax.numpy as jnp
from jax import lax
from jax.experimental import pallas as pl
from jax.experimental.pallas import tpu as pltpu
from jax.sharding import PartitionSpec as P

MESH = pl.DeviceIdType.MESH
BF = jnp.bfloat16
F32 = jnp.float32
VMEM = pltpu.VMEM
DMA = pltpu.SemaphoreType.DMA

TAB, COL, CORES, NZ, NY = 64, 4, 2, 8, 4
F, D, MAPS, ITEMS, SLOTS = 64, 48, 32, 4, 2
DL = D // COL
SAMP = 128
ROWS = SLOTS * DL
NB, BW = DL // 2, 2 * SAMP
HALF = F // 2
SCALE = D ** -0.5


def dot(a, b):
    return jnp.dot(a, b, preferred_element_type=F32)


def dot_nt(a, b):
    return lax.dot_general(a, b, (((1,), (1,)), ((), ())), preferred_element_type=F32)


def iota(shape, axis):
    return lax.broadcasted_iota(jnp.int32, shape, axis)


def send(src, dst, ssem, rsem, where):
    copy = pltpu.make_async_remote_copy(
        src_ref=src, dst_ref=dst, send_sem=ssem, recv_sem=rsem, device_id=where, device_id_type=MESH
    )
    copy.start()


def wait_send(src, dst, ssem, rsem, where):
    pltpu.make_async_remote_copy(
        src_ref=src, dst_ref=dst, send_sem=ssem, recv_sem=rsem, device_id=where, device_id_type=MESH
    ).wait_send()


def wait_recv(src, dst, ssem, rsem, where):
    pltpu.make_async_remote_copy(
        src_ref=src, dst_ref=dst, send_sem=ssem, recv_sem=rsem, device_id=where, device_id_type=MESH
    ).wait_recv()


def greet(me, col):
    barrier = pltpu.get_barrier_semaphore()

    def along_tab(k, _):
        pl.semaphore_signal(
            barrier, inc=1, device_id={"tab": lax.rem(me + k, TAB)}, device_id_type=MESH
        )
        return 0

    lax.fori_loop(1, TAB, along_tab, 0)
    for k in range(1, COL):
        pl.semaphore_signal(
            barrier, inc=1, device_id={"col": lax.rem(col + k, COL)}, device_id_type=MESH
        )
    return barrier


def gather_kernel(bag, lengths, cot, recv, up, snd, cots, ssem, rsem, csend, crecv, lsem):
    me = lax.axis_index("tab")
    col = lax.axis_index("col")
    barrier = greet(me, col)

    def pool(dst, _):
        at = pl.ds(pl.multiple_of(dst * SAMP, SAMP), SAMP)
        halves = []
        for slot in range(SLOTS):
            count = lengths[pl.ds(slot, 1), at]
            total = jnp.zeros((DL, SAMP), F32)
            for item in range(ITEMS):
                value = bag[slot, item, :, at].astype(F32)
                total = total + jnp.where(count > item, value, 0.0)
            halves.append(total)
        snd[dst] = jnp.concatenate(halves, axis=0).astype(BF)
        return 0

    lax.fori_loop(0, TAB, pool, 0)
    cots[col] = cot[...]
    pl.semaphore_wait(barrier, TAB - 1 + COL - 1)
    for k in range(1, COL):
        to = lax.rem(col + k, COL)
        send(cots.at[col], cots.at[col], csend.at[k], crecv.at[col], {"col": to})

    def issue(k, _):
        to = lax.rem(me + k, TAB)
        send(snd.at[to], recv.at[me], ssem.at[to], rsem.at[me], {"tab": to})
        return 0

    lax.fori_loop(1, TAB, issue, 0)
    own = pltpu.make_async_copy(snd.at[me], recv.at[me], lsem)
    own.start()
    for k in range(1, COL):
        to = lax.rem(col + k, COL)
        wait_recv(cots.at[to], cots.at[to], csend.at[k], crecv.at[to], {"col": to})
    wide = jnp.concatenate([cots[c] for c in range(COL)], axis=1)
    up[...] = (wide.astype(F32) * SCALE).astype(BF)
    own.wait()

    def drain(k, _):
        to = lax.rem(me + k, TAB)
        wait_send(snd.at[to], recv.at[me], ssem.at[to], rsem.at[me], {"tab": to})
        wait_recv(snd.at[to], recv.at[to], ssem.at[to], rsem.at[to], {"tab": to})
        return 0

    lax.fori_loop(1, TAB, drain, 0)
    for k in range(1, COL):
        to = lax.rem(col + k, COL)
        wait_send(cots.at[col], cots.at[col], csend.at[k], crecv.at[col], {"col": to})


def cross_kernel(
    fslot, recv, up, f1, f2, table, grads, pooled, za, lz, hot, es, egs, ef, tw, hf, hg, eg, zy, acc, pacc
):
    lane = iota((MAPS, 2 * F), 1)
    even = (lane < F).astype(BF)
    odd = (lane >= F).astype(BF)
    for t in range(HALF):
        first = f1[:, 2 * F * t : 2 * F * (t + 1)]
        second = f2[:, 2 * F * (t // 2) : 2 * F * (t // 2 + 1)]
        za[t, 0:32] = first * even
        za[t, 32:64] = first * odd
        za[t, 64:96] = second * (odd if t % 2 else even)
        za[t, 96:128] = jnp.zeros((MAPS, 2 * F), BF)
    zy[...] = jnp.zeros(zy.shape, BF)
    acc[...] = jnp.zeros(acc.shape, F32)
    pacc[...] = jnp.zeros(pacc.shape, F32)
    fold = (iota((F, 2 * F), 0) == lax.rem(iota((F, 2 * F), 1), F)).astype(F32).astype(BF)
    for q in range(8):
        part = za[4 * q : 4 * q + 4].reshape(512, 2 * F)
        lz[:, 512 * q : 512 * (q + 1)] = dot_nt(fold, part).astype(BF)

    fs = fslot[...]
    diag = iota((F, F), 0) == iota((F, F), 1)
    fcol = jnp.sum(jnp.where(diag, jnp.broadcast_to(fs, (F, F)), 0).astype(F32), axis=1, keepdims=True)
    fcol = fcol.astype(jnp.int32) * DL
    slot_row = iota((F, TAB * ROWS), 1)
    for d in range(DL):
        hot[pl.ds(F * d, F), :] = (slot_row == fcol + d).astype(F32).astype(BF)
    for q in range(3):
        got = dot(hot[pl.ds(256 * q, 256), :], recv[...]).astype(BF)
        for k in range(2):
            es[2 * q + k] = jnp.concatenate(
                [got[128 * k : 128 * k + 64], got[128 * k + 64 : 128 * k + 128]], axis=1
            )

    u = up[...].astype(F32)
    u = jnp.concatenate([u, u], axis=1)
    u1, u2 = u[:MAPS], u[MAPS:]
    r = iota((F, F), 0)
    source = 32 * (lax.rem(r, 16) // 8) + 8 * (r // 16) + lax.rem(r, 8)
    perm = (source == iota((F, F), 1)).astype(F32).astype(BF)

    def block(b, _):
        e = es[b]
        ef[...] = e.astype(F32)
        ee = jnp.concatenate([e, e], axis=0)
        for q in range(8):
            part = za[4 * q : 4 * q + 4].reshape(512, 2 * F)
            tw[4 * q : 4 * q + 4] = dot(part, ee).reshape(4, 128, BW)

        def first(t, m1):
            m1 = m1 + tw[t, 0:32] * ef[pl.ds(2 * t, 1)] + tw[t, 32:64] * ef[pl.ds(2 * t + 1, 1)]
            hg[pl.ds(t, 1)] = jnp.sum(tw[t, 64:96] * u2, axis=0, keepdims=True)
            return m1

        m1 = lax.fori_loop(0, HALF, first, jnp.zeros((MAPS, BW), F32), unroll=4)
        hf[...] = m1.astype(BF).astype(F32)
        lg = (u1 + hg[...]).astype(BF).astype(F32)

        def second(t, m2):
            hrow = hf[pl.ds(t, 1)]
            m2 = m2 + tw[t, 64:96] * hrow
            eg[pl.ds(2 * t, 1)] = jnp.sum(tw[t, 0:32] * lg, axis=0, keepdims=True)
            eg[pl.ds(2 * t + 1, 1)] = jnp.sum(tw[t, 32:64] * lg, axis=0, keepdims=True)
            zy[t, 0:32] = (lg * ef[pl.ds(2 * t, 1)]).astype(BF)
            zy[t, 32:64] = (lg * ef[pl.ds(2 * t + 1, 1)]).astype(BF)
            zy[t, 64:96] = (u2 * hrow).astype(BF)
            return m2

        m2 = lax.fori_loop(0, HALF, second, jnp.zeros((MAPS, BW), F32), unroll=4)
        pacc[0:MAPS] += m1
        pacc[MAPS:] += m2
        eperm = dot(perm, e).astype(BF)
        e2 = jnp.concatenate([e, eperm], axis=0)
        low = lax.rem(iota((F, 512), 1), 128) < F
        back = eg[...]
        for q in range(8):
            part = zy[4 * q : 4 * q + 4].reshape(512, BW)
            back = back + dot(lz[:, 512 * q : 512 * (q + 1)], part)
            both = dot_nt(e2, part)
            acc[:, 512 * q : 512 * (q + 1)] += jnp.where(low, both[:F], both[F:])
        back = back.astype(BF)
        egs[pl.ds(pl.multiple_of(128 * b, 128), 64)] = back[:, :SAMP]
        egs[pl.ds(pl.multiple_of(128 * b + 64, 64), 64)] = back[:, SAMP:]
        return 0

    lax.fori_loop(0, NB, block, 0)
    pooled[...] = (pacc[:, :SAMP] + pacc[:, SAMP:]) * SCALE
    grads[...] = acc[...].astype(BF)
    two = jnp.concatenate([fs, fs], axis=1) * DL + (iota((1, 2 * F), 1) >= F).astype(jnp.int32)
    for q in range(3):
        row = iota((512, 2 * F), 0) + 512 * q
        hots = [(row == two + 2 * k).astype(F32).astype(BF) for k in range(NB)]
        table[pl.ds(512 * q, 512), :] = dot(jnp.concatenate(hots, axis=1), egs[...]).astype(BF)


def scatter_kernel(
    table, grads, pooled, out, g1, g2, pout,
    back, xr, yr, zr, pr, ysend, fin, ssem, rsem, xs, xv, ps, pv, ys, yv, zs, zv, lsem,
):
    me = lax.axis_index("tab")
    col = lax.axis_index("col")
    core = lax.rem(me, CORES)
    z = lax.rem(me // CORES, NZ)
    y = me // (CORES * NZ)
    barrier = greet(me, col)
    pl.semaphore_wait(barrier, TAB - 1 + COL - 1)

    for k in range(1, COL):
        to = lax.rem(col + k, COL)
        rows = pl.ds(pl.multiple_of(16 * to, 16), 16)
        send(grads.at[rows], xr.at[col], xs.at[k], xv.at[col], {"col": to})
        send(pooled, pr.at[col], ps.at[k], pv.at[col], {"col": to})

    def issue(k, _):
        to = lax.rem(me + k, TAB)
        send(table.at[to], back.at[me], ssem.at[to], rsem.at[me], {"tab": to})
        return 0

    lax.fori_loop(1, TAB, issue, 0)
    own = pltpu.make_async_copy(table.at[me], back.at[me], lsem)
    own.start()

    xr[col] = grads[pl.ds(pl.multiple_of(16 * col, 16), 16)]
    pr[col] = pooled[...]
    for k in range(1, COL):
        to = lax.rem(col + k, COL)
        wait_recv(xr.at[to], xr.at[to], xs.at[k], xv.at[to], {"col": to})
    for c in range(NY):
        at = pl.ds(1024 * c, 1024)
        ysend[c] = (
            (xr[0, :, at].astype(F32) + xr[1, :, at].astype(F32))
            + (xr[2, :, at].astype(F32) + xr[3, :, at].astype(F32))
        )
    for k in range(1, NY):
        to = lax.rem(y + k, NY)
        send(ysend.at[to], yr.at[y], ys.at[k], yv.at[y], {"tab": (to * NZ + z) * CORES + core})
    yr[y] = ysend[y]
    for k in range(1, COL):
        to = lax.rem(col + k, COL)
        wait_recv(pr.at[to], pr.at[to], ps.at[k], pv.at[to], {"col": to})
    total = (pr[0] + pr[1]) + (pr[2] + pr[3])
    mine = jnp.zeros((2 * MAPS, SAMP // COL), F32)
    for c in range(COL):
        mine = mine + jnp.where(col == c, total[:, 32 * c : 32 * c + 32], 0.0)
    pout[...] = mine
    for k in range(1, NY):
        to = lax.rem(y + k, NY)
        wait_recv(yr.at[to], yr.at[to], ys.at[k], yv.at[to], {"tab": (to * NZ + z) * CORES + core})
    for c in range(NZ):
        at = pl.ds(128 * c, 128)
        fin[c] = (yr[0, :, at] + yr[1, :, at]) + (yr[2, :, at] + yr[3, :, at])
    group = NZ * CORES
    place = z * CORES + core
    base = y * group
    for k in range(1, group):
        to = lax.rem(place + k, group)
        send(fin.at[to // CORES], zr.at[place], zs.at[k], zv.at[place], {"tab": base + to})
    zr[place] = fin[z]
    for k in range(1, group):
        to = lax.rem(place + k, group)
        wait_recv(zr.at[to], zr.at[to], zs.at[k], zv.at[to], {"tab": base + to})
    parts = [zr[k] for k in range(group)]
    while len(parts) > 1:
        parts = [parts[i] + parts[i + 1] for i in range(0, len(parts), 2)]
    done = parts[0] * (8192 ** -0.5)
    swapped = jnp.transpose(jnp.concatenate([done, jnp.zeros((112, 128), F32)], axis=0))
    g1[...] = jnp.where(core == 0, swapped[0:32, 0:16], swapped[32:64, 0:16])
    g2[...] = jnp.where(core == 0, swapped[64:96, 0:8], swapped[64:96, 8:16])

    own.wait()

    def drain(k, _):
        to = lax.rem(me + k, TAB)
        wait_send(table.at[to], back.at[me], ssem.at[to], rsem.at[me], {"tab": to})
        wait_recv(table.at[to], back.at[to], ssem.at[to], rsem.at[to], {"tab": to})
        return 0

    lax.fori_loop(1, TAB, drain, 0)

    def place_out(src, _):
        at = pl.ds(pl.multiple_of(src * SAMP, SAMP), SAMP)
        value = back[src].astype(F32)
        out[0, :, at] = value[:DL].astype(BF)
        out[1, :, at] = value[DL:].astype(BF)
        return 0

    lax.fori_loop(0, TAB, place_out, 0)
    for k in range(1, COL):
        to = lax.rem(col + k, COL)
        rows = pl.ds(pl.multiple_of(16 * to, 16), 16)
        wait_send(grads.at[rows], xr.at[col], xs.at[k], xv.at[col], {"col": to})
        wait_send(pooled, pr.at[col], ps.at[k], pv.at[col], {"col": to})
    for k in range(1, NY):
        to = lax.rem(y + k, NY)
        wait_send(ysend.at[to], yr.at[y], ys.at[k], yv.at[y], {"tab": (to * NZ + z) * CORES + core})
    for k in range(1, group):
        to = lax.rem(place + k, group)
        wait_send(fin.at[to // CORES], zr.at[place], zs.at[k], zv.at[place], {"tab": base + to})


def vmem():
    return pl.BlockSpec(memory_space=VMEM)


def per_device(bag_items, lengths, field_slot, filter_one, filter_two, cotangent):
    shape = jax.ShapeDtypeStruct
    recv, up = pl.pallas_call(
        gather_kernel,
        out_shape=(shape((TAB, ROWS, SAMP), BF), shape((2 * MAPS, SAMP), BF)),
        in_specs=[vmem()] * 3,
        out_specs=[vmem()] * 2,
        scratch_shapes=[
            VMEM((TAB, ROWS, SAMP), BF),
            VMEM((COL, 2 * MAPS, SAMP // COL), BF),
            DMA((TAB,)), DMA((TAB,)), DMA((COL,)), DMA((COL,)), DMA,
        ],
        compiler_params=pltpu.CompilerParams(collective_id=0, has_side_effects=True),
        name="gather",
    )(bag_items, lengths, cotangent)
    table, grads, pooled = pl.pallas_call(
        cross_kernel,
        out_shape=(shape((TAB * ROWS, SAMP), BF), shape((F, 4096), BF), shape((2 * MAPS, SAMP), F32)),
        in_specs=[vmem()] * 5,
        out_specs=[vmem()] * 3,
        scratch_shapes=[
            VMEM((HALF, 128, 2 * F), BF),
            VMEM((F, 4096), BF),
            VMEM((DL * F, TAB * ROWS), BF),
            VMEM((NB, F, BW), BF),
            VMEM((DL * F, SAMP), BF),
            VMEM((F, BW), F32),
            VMEM((HALF, 128, BW), F32),
            VMEM((MAPS, BW), F32),
            VMEM((MAPS, BW), F32),
            VMEM((F, BW), F32),
            VMEM((HALF, 128, BW), BF),
            VMEM((F, 4096), F32),
            VMEM((2 * MAPS, BW), F32),
        ],
        name="cross",
    )(field_slot.reshape(1, F), recv.reshape(TAB * ROWS, SAMP), up, filter_one, filter_two)
    out, g1, g2, pout = pl.pallas_call(
        scatter_kernel,
        out_shape=(
            shape((SLOTS, DL, TAB * SAMP), BF),
            shape((MAPS, 16), F32),
            shape((MAPS, 8), F32),
            shape((2 * MAPS, SAMP // COL), F32),
        ),
        in_specs=[vmem()] * 3,
        out_specs=[vmem()] * 4,
        scratch_shapes=[
            VMEM((TAB, ROWS, SAMP), BF),
            VMEM((COL, 16, 4096), BF),
            VMEM((NY, 16, 1024), F32),
            VMEM((NZ * CORES, 16, 128), F32),
            VMEM((COL, 2 * MAPS, SAMP), F32),
            VMEM((NY, 16, 1024), F32),
            VMEM((NZ, 16, 128), F32),
            DMA((TAB,)), DMA((TAB,)),
            DMA((COL,)), DMA((COL,)), DMA((COL,)), DMA((COL,)),
            DMA((NY,)), DMA((NY,)), DMA((NZ * CORES,)), DMA((NZ * CORES,)), DMA,
        ],
        compiler_params=pltpu.CompilerParams(collective_id=1, has_side_effects=True),
        name="scatter",
    )(table.reshape(TAB, ROWS, SAMP), grads, pooled)
    return pout, g1, g2, out


def solution(mesh):
    in_specs = (P("tab", None, "col", None), P("tab", None), P(), P(), P(), P(None, ("tab", "col")))
    out_specs = (
        P(None, ("tab", "col")),
        P(None, ("tab", "col")),
        P(None, ("tab", "col")),
        P("tab", "col", None),
    )
    return jax.shard_map(
        per_device, mesh=mesh, in_specs=in_specs, out_specs=out_specs, check_vma=False
    )
```

time: 1480 us -> 90.4 us (0.06)
  waiting for transfers between devices: 1290 us -> 0 us
  Pallas kernels: 0 us -> 77.9 us
  other arithmetic: 55.8 us -> 0 us
  local copies, waits for them, and re-layouts: 45.9 us -> 11.4 us
  matrix products: 24.1 us -> 0 us
  starting transfers between devices: 22.6 us -> 0 us
  between operations: 15.7 us -> 0.65 us
    unnamed x6 -> x0, waiting for transfers between devices: 1290 us -> none
    pallas_call x0 -> x3, Pallas kernels: none -> 77.9 us  [the longest x1 31.6 us: per_device(): pl.pallas_call(scatter_kernel, out_shape=(shape((SLOTS, DL, TAB * SAMP),...]
    reduce_sum x11 -> x0, other arithmetic: 40.9 us -> none  [the longest x3 26.5 us: cross_block(): jnp.sum(pair_grad_one * first_float[None], axis=1)]
    convert_element_type x7 -> x0, local copies, waits for them, and re-layouts: 30.4 us -> none  [the longest x3 21.2 us: cross_block(): pair_grad_one.reshape(fields, fields, columns).astype(jnp.float32)]
    dot_general x18 -> x0, matrix products: 24.1 us -> none  [the longest x3 9.73 us: cross_block(): lax.dot_general(filter_one, lower_grad, (((0,), (0,)), ((), ())), preferr...]
    all_to_all x2 -> x0, starting transfers between devices: 22.5 us -> none  [the longest x1 13.1 us: per_device(): lax.all_to_all(per_owner, 'tab', split_axis=2, concat_axis=0, tiled=True)]
  transfers between devices with their start and end apart: 5 -> 0, of which waited for: 3 -> 0; matrix products, arithmetic and copies ran while one was open for 1% -> 0% of each run, Pallas kernels for 0% -> 0%
where the time goes in v1:
time: 90.4 us; the launch traced here: 90 us
  Pallas kernels  77.9 us (86%)
  local copies, waits for them, and re-layouts  11.4 us (13%)
    pallas_call x1, Pallas kernels, per_device(): pl.pallas_call(scatter_kernel, out_shape=(shape((SLOTS, DL, TAB * SAMP),...  31.6 us
    pallas_call x1, Pallas kernels, per_device(): pl.pallas_call(gather_kernel, out_shape=(shape((TAB, ROWS, SAMP), BF), sh...  25.7 us
    pallas_call x1, Pallas kernels, per_device(): pl.pallas_call(cross_kernel, out_shape=(shape((TAB * ROWS, SAMP), BF), sh...  20.6 us
    unnamed x6, local copies, waits for them, and re-layouts  11.4 us

profile of v1, /device:TPU:1, one launch (start us, length us, event | category | flops | bytes accessed | tf_op | source)
XLA Modules:
  0.0 90.0 jit_solution(13124278278723428646)
XLA Ops:
  0.6 1.4 %copy.11.cot = bf16[64,32]{1,0:T(8,128)(2,1)} copy(bf16[64,32]{0,1:T(8,128)(2,1)} %param.11) | data formatting | bytes 8192 | tf_op args[5]
  2.0 3.6 %copy.10.bag = bf16[2,4,12,8192]{3,2,1,0:T(8,128)(2,1)} copy(bf16[2,4,12,8192]{3,1,2,0:T(4,128)(2,1)} %param.6) | data formatting | bytes 3145728 | tf_op args[0]
  5.7 25.7 %gather.1 = (bf16[64,24,128]{2,1,0:T(8,128)(2,1)}, bf16[64,128]{1,0:T(8,128)(2,1)}) custom-call(bf16[2,4,12,8192]{3,2,1,0:T(8,128)(2,1)} %copy.10.bag, s32[2,8192]{1,0:T(2,128)} %lengths.1, bf16[64,32]{1,0:T(8,128)(2,1)} %copy.11.cot), custom_call_target="tpu_custom_call" | custom-call | tf_op jit(solution)/shard_map/gather/pallas_call | solution.py:333
  31.4 20.6 %cross.1 = (bf16[1536,128]{1,0:T(8,128)(2,1)}, bf16[64,4096]{1,0:T(8,128)(2,1)}, f32[64,128]{1,0:T(8,128)}) custom-call(s32[1,64]{1,0:T(1,128)} %bitcast.5, bf16[1536,128]{1,0:T(8,128)(2,1)} %bitcast.4, bf16[64,128]{1,0:T(8,128)(2,1)} %get-tuple-element.14.up, bf16[32,4096]{1,0:T(8,128)(2,1)} %f1.1, bf16[32,2048]{1,0:T(8,128)(2,1)} %f2.1), custom_call_target="tpu_custom_call" | custom-call | tf_op jit(solution)/shard_map/cross/pallas_call | solution.py:346
  52.0 31.6 %scatter.1 = (bf16[2,12,8192]{2,1,0:T(8,128)(2,1)}, f32[32,16]{1,0:T(8,128)}, f32[32,8]{1,0:T(8,128)}, f32[64,32]{1,0:T(8,128)}) custom-call(bf16[64,24,128]{2,1,0:T(8,128)(2,1)} %bitcast.3, bf16[64,4096]{1,0:T(8,128)(2,1)} %get-tuple-element.16.grads, f32[64,128]{1,0:T(8,128)} %get-tuple-element.17.pooled), custom_call_target="tpu_custom_call" | custom-call | tf_op jit(solution)/shard_map/scatter/pallas_call | solution.py:368
  83.6 1.4 %copy.12 = f32[64,32]{0,1:T(8,128)} copy(f32[64,32]{1,0:T(8,128)} %get-tuple-element.22) | data formatting | bytes 16384
  85.0 1.4 %copy.14 = f32[32,8]{0,1:T(8,128)} copy(f32[32,8]{1,0:T(8,128)} %get-tuple-element.24) | data formatting | bytes 2048
  86.4 1.4 %copy.13 = f32[32,16]{0,1:T(8,128)} copy(f32[32,16]{1,0:T(8,128)} %get-tuple-element.23) | data formatting | bytes 4096
  87.8 2.2 %copy.15 = bf16[2,12,8192]{2,0,1:T(2,128)(2,1)} copy(bf16[2,12,8192]{2,1,0:T(8,128)(2,1)} %get-tuple-element.25) | data formatting | bytes 786432
